TPU v7x, 512 devices: a whole 4x4x16 slice. The times are simulated.
512 devices in a mesh: dom: 128 (over x, y_hi, z), rel: 4 (over y_lo, core).
Axes of the slice: x: 4, y: 4 (y_hi: 2, y_lo: 2; y = y_hi * 2 + y_lo), z: 16, core: 2. Of those that a mesh axis runs over, the one named last changes fastest.
Arguments:
- emb: float32 [32768, 400], P('dom'), may hold values from -1.2 to 1.2
- emb_state: float32 [32768], P('dom'), may hold values from 0.02 to 2
- rel_weight: float32 [32, 400], P('rel'), may hold values from 0.5 to 1.5
- rel_state: float32 [32], P('rel'), may hold values from 1 to 1000
- swap_mask: int32 [1], replicated, may hold values from 1 to 127
- src_rows: int32 [4, 65536], P('rel', 'dom'), may hold values from 0 to 255
- dst_rows: int32 [4, 65536], P('rel', 'dom'), may hold values from 0 to 255
- tile_rel: int32 [4, 512], P('rel', 'dom'), may hold values from 0 to 7
- live_tiles: int32 [4, 128], P('rel', 'dom'), may hold values from 1 to 4, as said below
- neg_tiles: int32 [4, 1024], P('rel', 'dom'), may hold values from 0 to 1
- bound_rows: int32 [32768], P('dom'), may hold values from 0 to 255
- band_src: int32 [4, 32768], P('rel', 'dom'), may hold values from 0 to 255
- band_dst: int32 [4, 32768], P('rel', 'dom'), may hold values from 0 to 255
- band_rel: int32 [4, 256], P('rel', 'dom'), may hold values from 0 to 7
Outputs:
- emb_new: float32 [32768, 400], P('dom')
- state_new: float32 [32768], P('dom')
- rel_new: float32 [32, 400], P('rel')
Inputs may be any that keep to these rules, and one draw needn't show every extreme that they name: `live_tiles`: each entry counts the leading edge tiles of one bucket that hold edges; some relation group and partition has all 4 tiles live in every draw. `swap_mask`: the same plan entry holds for every partition, so pairs are mutual.
All inputs are finite; a program needn't handle non-finite values.
Results may differ from a plain program's by a relative error of at most 0.0029.
Values may be sent and summed in bfloat16 or wider, within the bound.
No kernel may reach another device: no remote copies, remote signals or barrier semaphores. Data moves between devices by JAX's collectives and lax.ppermute only.
A program may use at most 64 MiB of HBM per device.

v0:
```python
import jax
import jax.numpy as jnp
from jax import lax
from jax.sharding import PartitionSpec as P

step_rate = 0.25


def from_partner(block, axis, distance):
    count = lax.axis_size(axis)
    route = []
    for low in range(count):
        high = low | 1 << distance
        if high != low and high < count:
            route += [(low, high), (high, low)]
    return lax.ppermute(block, axis, route)


def padded_2(block, sides, width):
    for axis, dim in sides:
        count = lax.axis_size(axis)
        forward = [(i, i + 1) for i in range(count - 1)]
        backward = [(target, source) for source, target in forward]
        low = lax.ppermute(
            lax.slice_in_dim(block, block.shape[dim] - width, None, axis=dim), axis, forward
        )
        high = lax.ppermute(lax.slice_in_dim(block, 0, width, axis=dim), axis, backward)
        block = jnp.concatenate([low, block, high], axis=dim)
    return block


def edge_terms(q, target, negs, valid):
    pos = jnp.sum(q.astype(jnp.float32) * target.astype(jnp.float32), axis=1)
    neg = jnp.einsum("ed,nd->en", q, negs, preferred_element_type=jnp.float32)
    dpos = -jax.nn.sigmoid(-pos) * valid
    dneg = (jax.nn.sigmoid(neg) * (valid / negs.shape[0])[:, None]).astype(jnp.bfloat16)
    dq = dpos[:, None] * target.astype(jnp.float32) + jnp.einsum(
        "en,nd->ed", dneg, negs, preferred_element_type=jnp.float32
    )
    dtarget = dpos[:, None] * q.astype(jnp.float32)
    dnegs = jnp.einsum("en,ed->nd", dneg, q, preferred_element_type=jnp.float32)
    return (dq, dtarget, dnegs)


def bit_set(mask, bit):
    return mask // (1 << bit) % 2 == 1


def keep_same(values):
    return values


def route_block(values, mask):
    levels = lax.axis_size("dom").bit_length() - 1
    for bit in range(levels):

        def route_moved(current, level=bit):
            return from_partner(current, "dom", level)

        values = lax.cond(bit_set(mask, bit), route_moved, keep_same, values)
    return values


def return_block(values, mask):
    levels = lax.axis_size("dom").bit_length() - 1
    for bit in range(levels):

        def return_moved(current, level=bit):
            return from_partner(current, "dom", level)

        values = lax.cond(bit_set(mask, bit), return_moved, keep_same, values)
    return values


def adagrad(table, state, grad):
    fresh = state + jnp.mean(grad * grad, axis=1)
    return (table - step_rate * grad / jnp.sqrt(fresh)[:, None], fresh)


def relation_onehot(ids, count, tile):
    per_edge = jnp.repeat(ids, tile)
    return (per_edge[:, None] == jnp.arange(count)[None, :]).astype(jnp.float32)


def body(
    emb,
    emb_state,
    rel_weight,
    rel_state,
    swap_mask,
    src_rows,
    dst_rows,
    tile_rel,
    live_tiles,
    neg_tiles,
    bound_rows,
    band_src,
    band_dst,
    band_rel,
):
    part_rows, width = emb.shape
    tile = 128
    group = 4
    rel_count = rel_weight.shape[0]
    bnd = bound_rows.shape[0] // 2
    part_tiles = part_rows // tile
    neg_ids = neg_tiles[0]
    mask = swap_mask[0]
    own_bf = emb.astype(jnp.bfloat16)
    far = route_block(own_bf, mask)
    rim = own_bf[bound_rows]
    padded = padded_2(rim, (("dom", 0),), bnd)
    near = jnp.concatenate([padded[:bnd], padded[-bnd:]], axis=0)
    pick = (neg_ids[:, None] == jnp.arange(part_tiles)[None, :]).astype(jnp.float32)
    negs = jnp.einsum(
        "np,prd->nrd",
        pick.astype(jnp.bfloat16),
        far.reshape(part_tiles, tile, width),
        preferred_element_type=jnp.float32,
    )
    negs = negs.astype(jnp.bfloat16).reshape(neg_ids.shape[0] * tile, width)
    tile_ids = tile_rel[0]
    tile_onehot = (tile_ids[:, None] == jnp.arange(rel_count)[None, :]).astype(jnp.float32)
    w_tiles = jnp.dot(tile_onehot, rel_weight, precision=lax.Precision.HIGHEST)
    live = live_tiles[0, 0]
    sources = src_rows[0]
    targets = dst_rows[0]

    def run_block(index, carry):
        own_grad, far_grad, neg_grad, rel_grad = carry
        w_edge = jnp.broadcast_to(w_tiles[:, None, :], (group, tile, width)).reshape(
            group * tile, width
        )
        valid = (index * group + jnp.arange(group * tile) // tile < live).astype(jnp.float32)
        rows = emb[sources]
        q = (rows * w_edge).astype(jnp.bfloat16)
        dq, dtarget, dnegs = edge_terms(q, far[targets], negs, valid)
        own_grad = own_grad.at[sources].add(dq * w_edge)
        far_grad = far_grad.at[targets].add(dtarget)
        rel_grad = rel_grad + jnp.einsum(
            "er,ed->rd",
            relation_onehot(tile_ids, rel_count, tile),
            dq * rows,
            precision=lax.Precision.HIGHEST,
        )
        return (own_grad, far_grad, neg_grad + dnegs, rel_grad)

    start = (
        jnp.zeros((part_rows, width), jnp.float32),
        jnp.zeros((part_rows, width), jnp.float32),
        jnp.zeros(negs.shape, jnp.float32),
        jnp.zeros((rel_count, width), jnp.float32),
    )
    blocks_live = (live + group - 1) // group
    own_grad, far_grad, neg_grad, rel_grad = lax.fori_loop(0, blocks_live, run_block, start)
    band_ids = band_rel[0]
    band_tiles = band_ids.shape[0]
    band_onehot = (band_ids[:, None] == jnp.arange(rel_count)[None, :]).astype(jnp.float32)
    w_band_tiles = jnp.dot(band_onehot, rel_weight, precision=lax.Precision.HIGHEST)
    w_band = jnp.broadcast_to(w_band_tiles[:, None, :], (band_tiles, tile, width)).reshape(
        band_tiles * tile, width
    )
    band_from = band_src[0]
    band_to = band_dst[0]
    band_rows = emb[band_from]
    band_q = (band_rows * w_band).astype(jnp.bfloat16)
    band_valid = jnp.ones((band_tiles * tile,), jnp.float32)
    dq, dtarget, dnegs = edge_terms(band_q, near[band_to], negs, band_valid)
    own_grad = own_grad.at[band_from].add(dq * w_band)
    neg_grad = neg_grad + dnegs
    rel_grad = rel_grad + jnp.einsum(
        "er,ed->rd",
        relation_onehot(band_ids, rel_count, tile),
        dq * band_rows,
        precision=lax.Precision.HIGHEST,
    )
    far_grad = far_grad + jnp.einsum(
        "np,nrd->prd",
        pick,
        neg_grad.reshape(neg_ids.shape[0], tile, width),
        precision=lax.Precision.HIGHEST,
    ).reshape(part_rows, width)
    near_grad = jnp.zeros((2 * bnd, width), jnp.float32).at[band_to].add(dtarget)
    padded_grad = padded_2(near_grad.astype(jnp.bfloat16), (("dom", 0),), bnd).astype(
        near_grad.dtype
    )
    returned = jnp.concatenate([padded_grad[:bnd], padded_grad[-bnd:]], axis=0)
    local = own_grad.at[bound_rows].add(returned)
    total_rel = lax.psum(rel_grad, "dom")
    rel_new = (
        rel_weight
        - step_rate
        * total_rel
        / jnp.sqrt(rel_state + jnp.mean(total_rel * total_rel, axis=1))[:, None]
    )
    whole_grad = local + return_block(far_grad, mask)
    full_grad = lax.psum(whole_grad, "rel")
    emb_new, state_new = adagrad(emb, emb_state, full_grad)
    return (emb_new, state_new, rel_new)


def solution(mesh):
    in_specs = (
        P("dom", None),
        P("dom"),
        P("rel", None),
        P("rel"),
        P(),
        P("rel", "dom"),
        P("rel", "dom"),
        P("rel", "dom"),
        P("rel", "dom"),
        P("rel", "dom"),
        P("dom"),
        P("rel", "dom"),
        P("rel", "dom"),
        P("rel", "dom"),
    )
    out_specs = (P("dom", None), P("dom"), P("rel", None))
    return jax.shard_map(body, mesh=mesh, in_specs=in_specs, out_specs=out_specs, check_vma=False)
```

profile of v0, /device:TPU:1, one launch (start us, length us, event | category | flops | bytes accessed | tf_op | source)
XLA Modules:
  0.0 930.4 jit_solution(13966147584618793165)
XLA Ops:
  7.2 1.2 copy.56
  8.5 1.2 gather_fusion.5
  10.4 1.3 collective-permute-start.15
  11.7 5.6 collective-permute-start.14
  18.9 7.7 conditional.14
  18.9 2.9 collective-permute-start
  21.8 4.8 collective-permute-done
  26.6 1.6 gather_fusion.2
  30.5 19.1 %conditional.15 = (bf16[256,400]{1,0:T(8,128)(2,1)}) conditional(s32[]{:T(128)} %convert_element_type.167, bf16[256,400]{1,0:T(8,128)(2,1)} %get-tuple-element.671, bf16[256,400]{1,0:T(8,128)(2,1)} %get-tuple-element.671), branch_computations={%region_2.3_spmd, %region_3.4_spmd} | conditional | bytes 1228848 | solution.py:60
  30.5 7.1 collective-permute-start.1
  37.5 11.3 %collective-permute-done.1 = bf16[256,400]{1,0:T(8,128)(2,1)S(1)} collective-permute-done((bf16[256,400]{1,0:T(8,128)(2,1)}, bf16[256,400]{1,0:T(8,128)(2,1)S(1)}, u32[]{:S(2)}, u32[]{:S(2)}) %collective-permute-start.1) | collective-permute-done | bytes 204832 | tf_op jit(solution)/shard_map/cond/branch_1_fun/ppermute | solution.py:16
  49.5 3.0 gather_fusion.3
  55.4 1.3 copy.47
  56.8 1.4 broadcast_in_dim.44
  58.2 33.8 %while.21 = (s32[]{:T(128)}, f32[256,400]{1,0:T(8,128)S(1)}, f32[256,400]{1,0:T(8,128)S(1)}, f32[1024,400]{0,1:T(8,128)}, f32[8,400]{1,0:T(8,128)S(1)}, /*index=...) while((s32[]{:T(128)}, f32[256,400]{1,0:T(8,128)S(1)}, ...), condition=%wide.region_18.19_spmd, body=%wide.region_15.18_spmd.sunk | while | flops 1283260032 | bytes 38448668 | solution.py:155
  58.2 1.4 broadcast_in_dim.79
  60.4 2.3 gather_fusion
  62.7 1.5 copy.88
  64.2 1.1 convert_multiply_fusion.5
  65.7 2.0 multiply_convert_fusion.3
  67.7 3.6 gather_fusion.1
  71.4 2.0 copy.89
  73.3 3.5 bitcast_multiply_fusion.6
  76.8 1.5 copy.90
  78.3 3.8 scatter_fusion
  82.1 1.5 copy.91
  83.6 3.8 scatter_fusion.1
  87.4 3.7 convolution_add_fusion.7
  95.0 1.5 multiply_convert_fusion.1
  96.5 1.4 fusion.14
  98.9 1.9 gather_fusion.6
  102.9 1.2 bitcast_multiply_fusion.3
  106.8 14.5 %conditional.21 = (f32[256,400]{1,0:T(8,128)S(1)}) conditional(s32[]{:T(128)} %convert_element_type.168, f32[256,400]{1,0:T(8,128)S(1)} %bitcast_add_fusion, f32[256,400]{1,0:T(8,128)S(1)} %bitcast_add_fusion), branch_computations={%region_19.20_spmd, %region_20.21_spmd} | conditional | bytes 2457648 | solution.py:71
  106.8 3.7 collective-permute-start.7
  110.6 10.8 %collective-permute-done.7 = f32[256,400]{1,0:T(8,128)S(1)} collective-permute-done((f32[256,400]{1,0:T(8,128)S(1)}, f32[256,400]{1,0:T(8,128)S(1)}, u32[]{:S(2)}, u32[]{:S(2)}) %collective-permute-start.7) | collective-permute-done | bytes 409632 | tf_op jit(solution)/shard_map/cond/branch_1_fun/ppermute | solution.py:16
  121.4 28.7 %conditional.22 = (f32[256,400]{1,0:T(8,128)S(1)}) conditional(s32[]{:T(128)} %convert_element_type.167, f32[256,400]{1,0:T(8,128)S(1)} %get-tuple-element.678, f32[256,400]{1,0:T(8,128)S(1)} %get-tuple-element.678), branch_computations={%region_21.22_spmd, %region_22.23_spmd} | conditional | bytes 2457648 | solution.py:71
  121.4 5.9 collective-permute-start.8
  127.3 22.7 %collective-permute-done.8 = f32[256,400]{1,0:T(8,128)S(1)} collective-permute-done((f32[256,400]{1,0:T(8,128)S(1)}, f32[256,400]{1,0:T(8,128)S(1)}, u32[]{:S(2)}, u32[]{:S(2)}) %collective-permute-start.8) | collective-permute-done | bytes 409632 | tf_op jit(solution)/shard_map/cond/branch_1_fun/ppermute | solution.py:16
  152.3 2.7 scatter_custom_fusion.3
  155.1 1.3 collective-permute-start.17
  156.4 4.6 collective-permute-start.16
  161.3 600.9 %psum.15 = f32[8,400]{1,0:T(8,128)S(1)} all-reduce(f32[8,400]{1,0:T(8,128)S(1)} %convolution_add_fusion.4), channel_id=1, replica_groups=mesh['dom'=128,'rel'=4] {'dom'}, use_global_device_ids=true, to_apply=%region_39.40 | all-reduce | flops 3200 | bytes 25600 | tf_op jit(solution)/shard_map/psum | solution.py:189
  762.2 1.1 add.286
  763.4 2.3 scatter_fusion.2
  766.9 2.3 scatter_custom_fusion.4
  770.8 149.0 %all-reduce.2.cloned.1.call-done = f32[256,400]{1,0:T(8,128)} async-done(((f32[256,400]{1,0:T(8,128)}), f32[256,400]{1,0:T(8,128)}) %all-reduce.2.cloned.1.call-update) | async-done | bytes 409616 | tf_op jit(solution)/shard_map/psum | solution.py:197
  919.8 1.2 multiply_reduce_fusion.1
  921.5 1.2 divide_subtract_fusion
  (123 shorter events, 23.9 us)
Async XLA Ops:
  7.2 1.3 copy-start.18
  7.2 912.6 %all-reduce.2.cloned.1.call-start = ((), (), s32[]{:S(2)}) async-start(), calls=%async_computation | async-start | bytes 1048576 | tf_op jit(solution)/shard_map/psum | solution.py:197
  8.5 18.0 %copy-start.14 = (s32[1,512]{1,0:T(1,128)S(1)}, s32[1,512]{1,0:T(1,128)}, u32[]{:S(2)}) copy-start(s32[1,512]{1,0:T(1,128)} %param.50) | copy-start | bytes 6148
  8.5 18.0 %copy-start.13 = (s32[1,512]{1,0:T(1,128)S(1)}, s32[1,512]{1,0:T(1,128)}, u32[]{:S(2)}) copy-start(s32[1,512]{1,0:T(1,128)} %param.49) | copy-start | bytes 6148
  10.4 87.5 %collective-permute-start.15 = (bf16[128,400]{1,0:T(8,128)(2,1)}, bf16[128,400]{1,0:T(8,128)(2,1)}, u32[]{:S(2)}, u32[]{:S(2)}) collective-permute-start(bf16[128,400]{1,0:T(8,128)(2,1)} %get-tuple-element.513), channel_id=1, source_target_pairs={{4,0},{8,4},{12,8},{16,12},{20,16},{24,20},{28,24},{32,28},{36,32}... | collective-permute-start | bytes 307208 | tf_op jit(solution)/shard_map/ppermute | solution.py:27
  11.7 86.2 %collective-permute-start.14 = (bf16[128,400]{1,0:T(8,128)(2,1)}, bf16[128,400]{1,0:T(8,128)(2,1)}, u32[]{:S(2)}, u32[]{:S(2)}) collective-permute-start(bf16[128,400]{1,0:T(8,128)(2,1)} %get-tuple-element.512), channel_id=1, source_target_pairs={{0,4},{4,8},{8,12},{12,16},{16,20},{20,24},{24,28},{28,32},{32,36}... | collective-permute-start | bytes 307208 | tf_op jit(solution)/shard_map/ppermute | solution.py:24
  18.9 7.7 collective-permute-start
  26.6 1.7 copy-start.22
  26.6 1.7 copy-start.15
  26.6 2.8 copy-start.16
  30.5 18.4 %collective-permute-start.1 = (bf16[256,400]{1,0:T(8,128)(2,1)}, bf16[256,400]{1,0:T(8,128)(2,1)S(1)}, u32[]{:S(2)}, u32[]{:S(2)}) collective-permute-start(bf16[256,400]{1,0:T(8,128)(2,1)} %param.3), channel_id=1, source_target_pairs={{0,8},{8,0},{4,12},{12,4},{16,24},{24,16},{20,28},{28,20},{32,40},... | collective-permute-start | bytes 614408 | tf_op jit(solution)/shard_map/cond/branch_1_fun/ppermute | solution.py:16
  52.5 1.4 copy-start.17
  54.3 0.9 copy-start.5
  58.2 33.8 %copy-start.19 = (s32[1,256]{1,0:T(1,128)S(1)}, s32[1,256]{1,0:T(1,128)}, u32[]{:S(2)}) copy-start(s32[1,256]{1,0:T(1,128)} %param.56) | copy-start | bytes 3076
  58.2 33.8 %copy-start.20 = (s32[1,256]{1,0:T(1,128)S(1)}, s32[1,256]{1,0:T(1,128)}, u32[]{:S(2)}) copy-start(s32[1,256]{1,0:T(1,128)} %param.55) | copy-start | bytes 3076
  64.2 1.5 copy-start.4
  65.3 2.4 copy-start.3
  87.4 3.8 copy-start
  93.1 1.9 copy-start.10
  93.1 3.4 copy-start.6
  98.9 3.5 copy-start.7
  101.9 1.0 copy-start.8
  102.9 2.0 copy-start.1
  106.8 14.5 %collective-permute-start.7 = (f32[256,400]{1,0:T(8,128)S(1)}, f32[256,400]{1,0:T(8,128)S(1)}, u32[]{:S(2)}, u32[]{:S(2)}) collective-permute-start(f32[256,400]{1,0:T(8,128)S(1)} %param.17), channel_id=1, source_target_pairs={{0,4},{4,0},{8,12},{12,8},{16,20},{20,16},{24,28},{28,24},{32,36},... | collective-permute-start | bytes 1228808 | tf_op jit(solution)/shard_map/cond/branch_1_fun/ppermute | solution.py:16
  121.4 28.6 %collective-permute-start.8 = (f32[256,400]{1,0:T(8,128)S(1)}, f32[256,400]{1,0:T(8,128)S(1)}, u32[]{:S(2)}, u32[]{:S(2)}) collective-permute-start(f32[256,400]{1,0:T(8,128)S(1)} %param.19), channel_id=1, source_target_pairs={{0,8},{8,0},{4,12},{12,4},{16,24},{24,16},{20,28},{28,20},{32,40},... | collective-permute-start | bytes 1228808 | tf_op jit(solution)/shard_map/cond/branch_1_fun/ppermute | solution.py:16
  150.1 1.1 copy-start.12
  150.2 0.8 copy-start.9
  151.3 9.7 %copy-start.11 = (f32[256,400]{0,1:T(8,128)S(1)}, f32[256,400]{0,1:T(8,128)}, u32[]{:S(2)}) copy-start(f32[256,400]{0,1:T(8,128)} %get-tuple-element.515) | copy-start | bytes 1228804
  155.1 610.8 %collective-permute-start.17 = (bf16[128,400]{1,0:T(8,128)(2,1)S(1)}, bf16[128,400]{1,0:T(8,128)(2,1)}, u32[]{:S(2)}, u32[]{:S(2)}) collective-permute-start(bf16[128,400]{1,0:T(8,128)(2,1)S(1)} %get-tuple-element.511), channel_id=1, source_target_pairs={{4,0},{8,4},{12,8},{16,12},{20,16},{24,20},{28,24},{32,28},{36,32}... | collective-permute-start | bytes 307208 | tf_op jit(solution)/shard_map/ppermute | solution.py:27
  156.4 609.5 %collective-permute-start.16 = (bf16[128,400]{1,0:T(8,128)(2,1)S(1)}, bf16[128,400]{1,0:T(8,128)(2,1)}, u32[]{:S(2)}, u32[]{:S(2)}) collective-permute-start(bf16[128,400]{1,0:T(8,128)(2,1)S(1)} %get-tuple-element.510), channel_id=1, source_target_pairs={{0,4},{4,8},{8,12},{12,16},{16,20},{20,24},{24,28},{28,32},{32,36}... | collective-permute-start | bytes 307208 | tf_op jit(solution)/shard_map/ppermute | solution.py:24
  765.7 4.4 copy-start.23
  765.7 155.2 %copy-start.21 = (f32[256]{0:T(256)S(1)}, f32[256]{0:T(256)}, u32[]{:S(2)}) copy-start(f32[256]{0:T(256)} %param.45) | copy-start | bytes 3076
  769.2 0.8 copy-start.2
Sparse Core Ops, SparseCore 0:
  770.2 149.5 all-reduce.1
where the time goes:
time: 932 us; the launch traced here: 930 us
  blocking collectives  601 us (64%)
  waiting for transfers between devices  199 us (21%)
  local copies, waits for them, and re-layouts  39.8 us (4%)
  starting transfers between devices  32.5 us (3%)
  other arithmetic  26.4 us (3%)
  between operations  16.1 us (2%)
  matrix products  15.7 us (2%)
    psum x1, blocking collectives, body(): total_rel = lax.psum(rel_grad, 'dom')  601 us
    psum x1, waiting for transfers between devices, body(): full_grad = lax.psum(whole_grad, 'rel')  149 us
    ppermute x4, waiting for transfers between devices, from_partner(): return lax.ppermute(block, axis, route)  49.5 us
    ppermute x4, starting transfers between devices, from_partner(): return lax.ppermute(block, axis, route)  19.6 us
  transfers between devices with their start and end apart: 9, of which 5 were waited for; matrix products, arithmetic and copies ran while one was open for 6% of the time, Pallas kernels for 0%

commit v1 on v0

--- a/solution.py
+++ b/solution.py
@@ -194,7 +194,7 @@
         / jnp.sqrt(rel_state + jnp.mean(total_rel * total_rel, axis=1))[:, None]
     )
     whole_grad = local + return_block(far_grad, mask)
-    full_grad = lax.psum(whole_grad, "rel")
+    full_grad = jnp.sum(lax.all_gather(whole_grad, "rel"), axis=0)
     emb_new, state_new = adagrad(emb, emb_state, full_grad)
     return (emb_new, state_new, rel_new)
 

time: 932 us -> 897 us (0.962)
  the two profiles are of different devices: /device:TPU:1 before, /device:TPU:8 now
where the time goes in v1:
time: 897 us; the launch traced here: 896 us
  blocking collectives  711 us (79%)
  waiting for transfers between devices  51.9 us (6%)
  local copies, waits for them, and re-layouts  42.5 us (5%)
  starting transfers between devices  30.3 us (3%)
  other arithmetic  28.8 us (3%)
  between operations  16 us (2%)
  matrix products  15.7 us (2%)
    psum x1, blocking collectives, body(): total_rel = lax.psum(rel_grad, 'dom')  711 us
    ppermute x4, waiting for transfers between devices, from_partner(): return lax.ppermute(block, axis, route)  51.9 us
  transfers between devices with their start and end apart: 9, of which 4 were waited for; matrix products, arithmetic and copies ran while one was open for 6% of the time, Pallas kernels for 0%

profile of v1, /device:TPU:8, one launch (start us, length us, event | category | flops | bytes accessed | tf_op | source)
XLA Modules:
  0.0 896.2 jit_solution(9574803074429486654)
XLA Ops:
  7.2 1.2 copy.72
  8.5 1.2 gather_fusion.5
  10.4 1.3 collective-permute-start.15
  11.7 5.2 collective-permute-start.14
  18.4 9.7 %conditional.14 = (bf16[256,400]{1,0:T(8,128)(2,1)}) conditional(s32[]{:T(128)} %convert_element_type.168, bf16[256,400]{1,0:T(8,128)(2,1)S(1)} %convert_element_type.169, bf16[256,400]{1,0:T(8,128)(2,1)S(1)} %convert_element_type.169), branch_computations={%region_0.1_spmd, %region_1.2_spmd} | conditional | bytes 819248 | solution.py:60
  18.4 3.2 collective-permute-start
  21.6 6.5 collective-permute-done
  28.2 1.6 gather_fusion.2
  30.9 17.8 %conditional.15 = (bf16[256,400]{1,0:T(8,128)(2,1)}) conditional(s32[]{:T(128)} %convert_element_type.167, bf16[256,400]{1,0:T(8,128)(2,1)} %get-tuple-element.686, bf16[256,400]{1,0:T(8,128)(2,1)} %get-tuple-element.686), branch_computations={%region_2.3_spmd, %region_3.4_spmd} | conditional | bytes 1228848 | solution.py:60
  30.9 5.9 collective-permute-start.1
  36.8 11.2 %collective-permute-done.1 = bf16[256,400]{1,0:T(8,128)(2,1)S(1)} collective-permute-done((bf16[256,400]{1,0:T(8,128)(2,1)}, bf16[256,400]{1,0:T(8,128)(2,1)S(1)}, u32[]{:S(2)}, u32[]{:S(2)}) %collective-permute-start.1) | collective-permute-done | bytes 204832 | tf_op jit(solution)/shard_map/cond/branch_1_fun/ppermute | solution.py:16
  48.7 3.0 gather_fusion.3
  54.6 1.3 copy.63
  56.0 1.4 broadcast_in_dim.44
  57.4 33.8 %while.21 = (s32[]{:T(128)}, f32[256,400]{1,0:T(8,128)S(1)}, f32[256,400]{1,0:T(8,128)S(1)}, f32[1024,400]{0,1:T(8,128)}, f32[8,400]{1,0:T(8,128)S(1)}, /*index=...) while((s32[]{:T(128)}, f32[256,400]{1,0:T(8,128)S(1)}, ...), condition=%wide.region_18.19_spmd, body=%wide.region_15.18_spmd.sunk | while | flops 1283260032 | bytes 38448668 | solution.py:155
  57.4 1.4 broadcast_in_dim.79
  59.5 2.3 gather_fusion
  61.9 1.5 copy.104
  64.9 2.0 multiply_convert_fusion.3
  66.9 3.6 gather_fusion.1
  70.6 2.0 copy.105
  72.5 3.5 bitcast_multiply_fusion.6
  76.0 1.5 copy.106
  77.5 3.8 scatter_fusion
  81.3 1.5 copy.107
  82.8 3.8 scatter_fusion.1
  86.6 3.7 convolution_add_fusion.7
  94.5 1.5 multiply_convert_fusion.1
  96.0 1.4 fusion.14
  98.5 1.9 gather_fusion.6
  102.5 1.2 bitcast_multiply_fusion.3
  105.2 1.6 fusion.32
  106.8 1.2 copy.76
  108.0 2.0 copy.71
  110.0 3.4 scatter_custom_fusion.3
  114.4 1.3 collective-permute-start.17
  115.7 5.2 collective-permute-start.16
  121.8 15.3 %conditional.21 = (f32[256,400]{1,0:T(8,128)}) conditional(s32[]{:T(128)} %convert_element_type.168, f32[256,400]{1,0:T(8,128)} %bitcast_add_fusion, f32[256,400]{1,0:T(8,128)} %bitcast_add_fusion), branch_computations={%region_19.20_spmd, %region_20.21_spmd} | conditional | bytes 2457648 | solution.py:71
  121.8 2.1 collective-permute-start.7
  123.9 12.4 %collective-permute-done.7 = f32[256,400]{1,0:T(8,128)S(1)} collective-permute-done((f32[256,400]{1,0:T(8,128)}, f32[256,400]{1,0:T(8,128)S(1)}, u32[]{:S(2)}, u32[]{:S(2)}) %collective-permute-start.7) | collective-permute-done | bytes 409632 | tf_op jit(solution)/shard_map/cond/branch_1_fun/ppermute | solution.py:16
  137.1 28.7 %conditional.22 = (f32[256,400]{1,0:T(8,128)}) conditional(s32[]{:T(128)} %convert_element_type.167, f32[256,400]{1,0:T(8,128)} %get-tuple-element.693, f32[256,400]{1,0:T(8,128)} %get-tuple-element.693), branch_computations={%region_21.22_spmd, %region_22.23_spmd} | conditional | bytes 2457648 | solution.py:71
  137.1 6.1 collective-permute-start.8
  143.2 21.8 %collective-permute-done.8 = f32[256,400]{1,0:T(8,128)S(1)} collective-permute-done((f32[256,400]{1,0:T(8,128)}, f32[256,400]{1,0:T(8,128)S(1)}, u32[]{:S(2)}, u32[]{:S(2)}) %collective-permute-start.8) | collective-permute-done | bytes 409632 | tf_op jit(solution)/shard_map/cond/branch_1_fun/ppermute | solution.py:16
  166.0 1.1 add.284
  167.1 2.3 scatter_fusion.2
  170.6 2.3 scatter_custom_fusion.4
  174.2 710.7 %psum.7 = f32[8,400]{1,0:T(8,128)S(1)} all-reduce(f32[8,400]{1,0:T(8,128)S(1)} %convolution_add_fusion.4), channel_id=1, replica_groups=mesh['dom'=128,'rel'=4] {'dom'}, use_global_device_ids=true, to_apply=%region_39.40 | all-reduce | flops 3200 | bytes 25600 | tf_op jit(solution)/shard_map/psum | solution.py:189
  885.7 1.9 reduce_sum.47
  (118 shorter events, 24.9 us)
Async XLA Ops:
  7.2 1.3 copy-start.15
  7.2 878.5 %all-gather.3.cloned.1.call-start = ((), (), s32[]{:S(2)}) async-start(), calls=%async_computation | async-start | bytes 2621440 | tf_op jit(solution)/shard_map/all_gather | solution.py:197
  8.5 19.6 %copy-start.11 = (s32[1,512]{1,0:T(1,128)S(1)}, s32[1,512]{1,0:T(1,128)}, u32[]{:S(2)}) copy-start(s32[1,512]{1,0:T(1,128)} %param.50) | copy-start | bytes 6148
  8.5 19.6 %copy-start.10 = (s32[1,512]{1,0:T(1,128)S(1)}, s32[1,512]{1,0:T(1,128)}, u32[]{:S(2)}) copy-start(s32[1,512]{1,0:T(1,128)} %param.49) | copy-start | bytes 6148
  10.4 87.0 %collective-permute-start.15 = (bf16[128,400]{1,0:T(8,128)(2,1)}, bf16[128,400]{1,0:T(8,128)(2,1)}, u32[]{:S(2)}, u32[]{:S(2)}) collective-permute-start(bf16[128,400]{1,0:T(8,128)(2,1)} %get-tuple-element.528), channel_id=1, source_target_pairs={{4,0},{8,4},{12,8},{16,12},{20,16},{24,20},{28,24},{32,28},{36,32}... | collective-permute-start | bytes 307208 | tf_op jit(solution)/shard_map/ppermute | solution.py:27
  11.7 85.7 %collective-permute-start.14 = (bf16[128,400]{1,0:T(8,128)(2,1)}, bf16[128,400]{1,0:T(8,128)(2,1)}, u32[]{:S(2)}, u32[]{:S(2)}) collective-permute-start(bf16[128,400]{1,0:T(8,128)(2,1)} %get-tuple-element.527), channel_id=1, source_target_pairs={{0,4},{4,8},{8,12},{12,16},{16,20},{20,24},{24,28},{28,32},{32,36}... | collective-permute-start | bytes 307208 | tf_op jit(solution)/shard_map/ppermute | solution.py:24
  18.4 9.7 %collective-permute-start = (bf16[256,400]{1,0:T(8,128)(2,1)S(1)}, bf16[256,400]{1,0:T(8,128)(2,1)}, u32[]{:S(2)}, u32[]{:S(2)}) collective-permute-start(bf16[256,400]{1,0:T(8,128)(2,1)S(1)} %param.1), channel_id=1, source_target_pairs={{0,4},{4,0},{8,12},{12,8},{16,20},{20,16},{24,28},{28,24},{32,36},... | collective-permute-start | bytes 614408 | tf_op jit(solution)/shard_map/cond/branch_1_fun/ppermute | solution.py:16
  28.2 1.7 copy-start.12
  28.2 1.7 copy-start.13
  30.9 17.1 %collective-permute-start.1 = (bf16[256,400]{1,0:T(8,128)(2,1)}, bf16[256,400]{1,0:T(8,128)(2,1)S(1)}, u32[]{:S(2)}, u32[]{:S(2)}) collective-permute-start(bf16[256,400]{1,0:T(8,128)(2,1)} %param.3), channel_id=1, source_target_pairs={{0,8},{8,0},{4,12},{12,4},{16,24},{24,16},{20,28},{28,20},{32,40},... | collective-permute-start | bytes 614408 | tf_op jit(solution)/shard_map/cond/branch_1_fun/ppermute | solution.py:16
  51.7 1.4 copy-start.14
  53.5 0.9 copy-start.5
  57.4 33.8 %copy-start.16 = (s32[1,256]{1,0:T(1,128)S(1)}, s32[1,256]{1,0:T(1,128)}, u32[]{:S(2)}) copy-start(s32[1,256]{1,0:T(1,128)} %param.56) | copy-start | bytes 3076
  57.4 33.8 %copy-start.17 = (s32[1,256]{1,0:T(1,128)S(1)}, s32[1,256]{1,0:T(1,128)}, u32[]{:S(2)}) copy-start(s32[1,256]{1,0:T(1,128)} %param.55) | copy-start | bytes 3076
  63.4 1.5 copy-start.4
  64.5 2.4 copy-start.3
  86.6 3.8 copy-start
  91.3 1.9 copy-start.19
  92.3 3.8 copy-start.6
  98.5 3.5 copy-start.7
  101.4 1.0 copy-start.8
  102.5 2.0 copy-start.1
  114.4 55.0 %collective-permute-start.17 = (bf16[128,400]{1,0:T(8,128)(2,1)S(1)}, bf16[128,400]{1,0:T(8,128)(2,1)}, u32[]{:S(2)}, u32[]{:S(2)}) collective-permute-start(bf16[128,400]{1,0:T(8,128)(2,1)S(1)} %get-tuple-element.526), channel_id=1, source_target_pairs={{4,0},{8,4},{12,8},{16,12},{20,16},{24,20},{28,24},{32,28},{36,32}... | collective-permute-start | bytes 307208 | tf_op jit(solution)/shard_map/ppermute | solution.py:27
  115.7 53.7 %collective-permute-start.16 = (bf16[128,400]{1,0:T(8,128)(2,1)S(1)}, bf16[128,400]{1,0:T(8,128)(2,1)}, u32[]{:S(2)}, u32[]{:S(2)}) collective-permute-start(bf16[128,400]{1,0:T(8,128)(2,1)S(1)} %get-tuple-element.525), channel_id=1, source_target_pairs={{0,4},{4,8},{8,12},{12,16},{16,20},{20,24},{24,28},{28,32},{32,36}... | collective-permute-start | bytes 307208 | tf_op jit(solution)/shard_map/ppermute | solution.py:24
  121.8 14.5 %collective-permute-start.7 = (f32[256,400]{1,0:T(8,128)}, f32[256,400]{1,0:T(8,128)S(1)}, u32[]{:S(2)}, u32[]{:S(2)}) collective-permute-start(f32[256,400]{1,0:T(8,128)} %param.17), channel_id=1, source_target_pairs={{0,4},{4,0},{8,12},{12,8},{16,20},{20,16},{24,28},{28,24},{32,36},... | collective-permute-start | bytes 1228808 | tf_op jit(solution)/shard_map/cond/branch_1_fun/ppermute | solution.py:16
  137.1 27.9 %collective-permute-start.8 = (f32[256,400]{1,0:T(8,128)}, f32[256,400]{1,0:T(8,128)S(1)}, u32[]{:S(2)}, u32[]{:S(2)}) collective-permute-start(f32[256,400]{1,0:T(8,128)} %param.19), channel_id=1, source_target_pairs={{0,8},{8,0},{4,12},{12,4},{16,24},{24,16},{20,28},{28,20},{32,40},... | collective-permute-start | bytes 1228808 | tf_op jit(solution)/shard_map/cond/branch_1_fun/ppermute | solution.py:16
  169.4 4.4 copy-start.9
  169.4 715.5 %copy-start.20 = (f32[8]{0:T(128)S(1)}, f32[8]{0:T(128)}, u32[]{:S(2)}) copy-start(f32[8]{0:T(128)} %param.47) | copy-start | bytes 100
  172.9 0.8 copy-start.2
  174.2 713.5 %copy-start.18 = (f32[256]{0:T(256)S(1)}, f32[256]{0:T(256)}, u32[]{:S(2)}) copy-start(f32[256]{0:T(256)} %param.45) | copy-start | bytes 3076
Sparse Core Ops, SparseCore 0:
  173.9 40.7 all-gather.2
